TPU v7x, 256 devices: a whole 4x4x8 slice. The times are simulated.
256 devices in a mesh: src: 8 (over y, core), tp: 16 (over x, z_hi), row: 2 (over z_lo).
Axes of the slice: x: 4, y: 4, z: 8 (z_hi: 4, z_lo: 2; z = z_hi * 2 + z_lo), core: 2. Of those that a mesh axis runs over, the one named last changes fastest.
Arguments:
- tokens: bfloat16 [8, 256, 8192], P('src', 'tp', 'row'), may hold values from -6 to 6
- coefficients: float32 [8, 8], replicated, may hold values from -2 to 2
- gate_weights: bfloat16 [8, 8192, 4096], P('src', 'row', 'tp'), may hold values from -0.0625 to 0.0625
- up_weights: bfloat16 [8, 8192, 4096], P('src', 'row', 'tp'), may hold values from -0.0625 to 0.0625
Outputs:
- hidden: bfloat16 [8, 256, 4096], P('src', 'row', 'tp')
All inputs are finite; a program needn't handle non-finite values.
Results may differ from a plain program's by a relative error of at most 0.0013.
Values may be sent and summed in bfloat16 or wider, within the bound.
A program may use at most 64 MiB of HBM per device.

v0:
```python
import jax
import jax.numpy as jnp
from jax import lax
from jax.sharding import PartitionSpec as P


def split_up(array, dim, devices):
    shape = array.shape
    tiles = array.reshape(*shape[:dim], devices, shape[dim] // devices, *shape[dim + 1 :])
    return jnp.moveaxis(tiles, dim, 0)


def sent_and_summed(array, axis, dim):
    tiles = split_up(array, dim, lax.axis_size(axis))
    arrived = lax.all_to_all(tiles, axis, split_axis=0, concat_axis=0, tiled=True)
    return arrived.sum(axis=0)


def shards(tokens, coefficients, gate_weights, up_weights):
    local_rows = tokens.shape[1]
    half_width = tokens.shape[2]
    candidates = coefficients.shape[0]
    sources = coefficients.shape[1]
    per_candidate = local_rows * lax.axis_size("tp")
    out_rows = per_candidate // lax.axis_size("row")
    own_source = lax.axis_index("src")
    picked = (jnp.arange(sources, dtype=jnp.int32) == own_source).astype(jnp.float32)
    own_factors = jnp.sum(coefficients * picked[None, :], axis=1)
    gate_local = gate_weights[0]
    up_local = up_weights[0]
    hidden_width = gate_local.shape[1]
    flat_tokens = tokens.reshape(local_rows, half_width)
    row_block = lax.all_gather(flat_tokens, ("src", "tp"), axis=0, tiled=True)
    row_count = row_block.shape[0]
    owner_ids = jnp.arange(row_count, dtype=jnp.int32) // per_candidate
    one_hot = (owner_ids[:, None] == jnp.arange(candidates, dtype=jnp.int32)[None, :]).astype(
        jnp.float32
    )
    factor = jnp.sum(one_hot * own_factors[None, :], axis=1)[:, None]
    gate_part = jnp.dot(row_block, gate_local, preferred_element_type=jnp.float32)
    up_part = jnp.dot(row_block, up_local, preferred_element_type=jnp.float32)
    collected = jnp.concatenate((gate_part, up_part), axis=1) * factor
    summed = sent_and_summed(collected, ("src", "row"), 0)
    hidden = (jax.nn.silu(summed[:, :hidden_width]) * summed[:, hidden_width:]).astype(jnp.bfloat16)
    return hidden.reshape(1, out_rows, hidden_width)


def solution(mesh):
    return jax.shard_map(
        shards,
        mesh=mesh,
        in_specs=(P("src", "tp", "row"), P(), P("src", "row", "tp"), P("src", "row", "tp")),
        out_specs=P("src", "row", "tp"),
        check_vma=False,
    )
```

profile of v0, /device:TPU:1, one launch (start us, length us, event | category | flops | bytes accessed | tf_op | source)
XLA Modules:
  0.0 212.2 jit_solution(2710372214216165005)
XLA Ops:
  6.5 0.0 copy-start
  6.5 0.0 all-gather.3.cloned.1.call-start
  6.5 0.7 all-gather.3.cloned.1.call-update
  7.3 0.8 multiply_reduce_fusion
  8.1 0.1 select_reduce_fusion
  8.2 123.5 %all-gather.3.cloned.1.call-done = bf16[1,2048,4096]{2,1,0:T(8,128)(2,1)} async-done(((bf16[1,16,4096]{2,1,0:T(8,128)(2,1)}), bf16[1,2048,4096]{2,1,0:T(8,128)(2,1)}) %all-gather.3.cloned.1.call-update) | async-done | bytes 16777232 | tf_op jit(solution)/shard_map/all_gather | solution.py:33
  131.7 0.0 copy-done
  131.7 0.0 copy-start.1
  131.7 0.0 copy-start.2
  131.7 8.3 %fusion = f32[16,128,256]{2,1,0:T(8,128)S(1)} fusion(bf16[16,128,4096]{2,1,0:T(8,128)(2,1)} %bitcast.15, bf16[1,4096,256]{2,1,0:T(8,128)(2,1)S(1)} %copy-done), kind=kOutput, calls=%fused_computation.1 | convolution fusion | flops 4294967296 | bytes 20971520 | tf_op jit(solution)/shard_map/dot_general | solution.py:41
  140.0 2.3 %copy-done.1 = bf16[1,2048,4096]{2,1,0:T(8,128)(2,1)S(1)} copy-done((bf16[1,2048,4096]{2,1,0:T(8,128)(2,1)S(1)}, bf16[1,2048,4096]{2,1,0:T(8,128)(2,1)}, u32[]{:S(2)}) %copy-start.1) | copy-done | bytes 16777240
  142.3 0.6 copy-done.2
  142.9 4.9 %fusion.2 = f32[16,128,256]{2,1,0:T(8,128)S(1)} fusion(bf16[16,128,4096]{2,1,0:T(8,128)(2,1)S(1)} %bitcast.16, bf16[1,4096,256]{2,1,0:T(8,128)(2,1)S(1)} %copy-done.2), kind=kOutput, calls=%fused_computation.3 | convolution fusion | flops 4294967296 | bytes 20971520 | tf_op jit(solution)/shard_map/dot_general | solution.py:40
  147.8 0.4 maximum_multiply_fusion
  148.2 53.9 %all_to_all.5 = f32[16,128,512]{2,1,0:T(8,128)} all-to-all(f32[16,128,512]{2,1,0:T(8,128)S(1)} %maximum_multiply_fusion), channel_id=1, replica_groups=mesh['src'=8,'tp'=16,'row'=2] {'src','row'}, dimensions={0} | all-to-all | bytes 8388608 | tf_op jit(solution)/shard_map/all_to_all | solution.py:15
  202.0 2.6 %reduce_sum.29 = f32[128,512]{1,0:T(8,128)S(1)} reduce(f32[16,128,512]{2,1,0:T(8,128)} %all_to_all.5, f32[]{:T(128)} %constant.28.clone.1), dimensions={0}, to_apply=%region_2.3 | reduce | flops 983040 | bytes 4456452 | tf_op jit(solution)/shard_map/reduce_sum | solution.py:16
  204.7 0.7 fusion.5
  (2 shorter events, 0.0 us)
Async XLA Ops:
  6.5 125.2 %copy-start = (bf16[1,4096,256]{2,1,0:T(8,128)(2,1)S(1)}, bf16[1,4096,256]{2,1,0:T(8,128)(2,1)}, u32[]{:S(2)}) copy-start(bf16[1,4096,256]{2,1,0:T(8,128)(2,1)} %param.7) | copy-start | bytes 6291460
  6.5 125.2 %all-gather.3.cloned.1.call-start = ((), (), s32[]{:S(2)}) async-start(), calls=%async_computation.1 | async-start | bytes 16908288 | tf_op jit(solution)/shard_map/all_gather | solution.py:33
  131.7 10.5 %copy-start.1 = (bf16[1,2048,4096]{2,1,0:T(8,128)(2,1)S(1)}, bf16[1,2048,4096]{2,1,0:T(8,128)(2,1)}, u32[]{:S(2)}) copy-start(bf16[1,2048,4096]{2,1,0:T(8,128)(2,1)} %all-gather.3.cloned.1.call-done) | copy-start | bytes 50331652
  131.7 11.1 %copy-start.2 = (bf16[1,4096,256]{2,1,0:T(8,128)(2,1)S(1)}, bf16[1,4096,256]{2,1,0:T(8,128)(2,1)}, u32[]{:S(2)}) copy-start(bf16[1,4096,256]{2,1,0:T(8,128)(2,1)} %param.6) | copy-start | bytes 6291460
Sparse Core Ops, SparseCore 0:
  10.9 120.7 all-gather.2
where the time goes:
time: 212 us
  waiting for transfers between devices  124 us (58%)
  blocking collectives  53.9 us (25%)
  between operations  13.4 us (6%)
  matrix products  13.2 us (6%)
  other arithmetic  4.6 us (2%)
  local copies, waits for them, and re-layouts  2.86 us (1%)
    all_gather x1, waiting for transfers between devices, shards(): row_block = lax.all_gather(flat_tokens, ('src', 'tp'), axis=0, tiled=True)  124 us
    all_to_all x1, blocking collectives, sent_and_summed(): lax.all_to_all(tiles, axis, split_axis=0, concat_axis=0, tiled=True)  53.9 us
    dot_general x1, matrix products, shards(): up_part = jnp.dot(row_block, up_local, preferred_element_type=jnp.float32)  8.28 us
    dot_general x1, matrix products, shards(): jnp.dot(row_block, gate_local, preferred_element_type=jnp.float32)  4.9 us
  transfers between devices with their start and end apart: 1, of which 1 were waited for; matrix products, arithmetic and copies ran while one was open for 0% of the time, Pallas kernels for 0%

commit v1 on v0

v1 whole, which is shorter than its diff:
```python
import jax
import jax.numpy as jnp
from jax import lax
from jax.experimental import pallas as pl
from jax.experimental.pallas import tpu as pltpu
from jax.sharding import PartitionSpec as P

MESH = pl.DeviceIdType.MESH
QUARTERS = (0, 3, 1, 2)


def mod4(value):
    return lax.rem(value, jnp.int32(4))


def kernel(
    tok_hbm, coef, gate_hbm, up_hbm, out_ref,
    tok, wts, part, r_sib, z_out, r_z, r_y2, r_y1,
    s_local, s_send, s_z, s_a, s_b, s_b0, s_sib, s_rsib, s_rz, s_ry2, s_ry1,
):
    src, tp, row = lax.axis_index("src"), lax.axis_index("tp"), lax.axis_index("row")
    y, c = lax.div(src, jnp.int32(2)), lax.rem(src, jnp.int32(2))
    x, zh = lax.div(tp, jnp.int32(4)), mod4(tp)
    first = x * (1 - c) + y * c
    last = y * (1 - c) + x * c

    def device(dx=0, dy=0, dz=0):
        return (2 * mod4(y + dy) + c, 4 * mod4(x + dx) + mod4(zh + dz), row)

    def on_a(step):
        return device(dx=step * (1 - c), dy=step * c)

    def on_b(step):
        return device(dx=step * c, dy=step * (1 - c))

    sibling = (2 * y + 1 - c, tp, row)
    partner = (src, tp, 1 - row)

    def slab(q, l, f):
        return ((c * 4 + q) * 4 + l) * 4 + f

    def shards(q, l, f=0, count=1):
        return tok.at[pl.ds(slab(q, l, f), count)]

    def send(ref, there, sem, to, kind=0):
        pltpu.make_async_remote_copy(
            src_ref=ref, dst_ref=there, send_sem=s_send.at[kind], recv_sem=sem, device_id=to, device_id_type=MESH
        ).start()

    def wait(ref, sem):
        pltpu.make_async_copy(ref, ref, sem).wait()

    own = pltpu.make_async_copy(tok_hbm, shards(zh, last, first), s_local.at[0])
    gate_in = pltpu.make_async_copy(gate_hbm.at[0], wts.at[:, pl.ds(0, 256)], s_local.at[1])
    up_in = pltpu.make_async_copy(up_hbm.at[0], wts.at[:, pl.ds(256, 256)], s_local.at[2])
    own.start()
    gate_in.start()
    up_in.start()

    barrier = pltpu.get_barrier_semaphore()
    greeted = [on_a(1), on_a(3), on_b(1), on_b(3), device(dz=1), device(dz=3), device(dz=2), sibling, partner]
    for one in greeted:
        pl.semaphore_signal(barrier, inc=1, device_id=one, device_id_type=MESH)
    own.wait()
    pl.semaphore_wait(barrier, len(greeted))

    qs = [mod4(zh + d) for d in QUARTERS]
    f_minus, f_plus, f_far = mod4(first + 3), mod4(first + 1), mod4(first + 2)
    l_minus, l_plus, l_far = mod4(last + 3), mod4(last + 1), mod4(last + 2)

    def send_a(k):
        one = shards(qs[k], last, first)
        send(one, one, s_a.at[k, 0], on_a(1))
        send(one, one, s_a.at[k, 1], on_a(3))

    def send_b_one(f):
        one = shards(qs[0], last, f)
        send(one, one, s_b.at[0, 0], on_b(1))
        send(one, one, s_b.at[0, 1], on_b(3))

    def send_sib(k, l):
        block = shards(qs[k], l, 0, 4)
        send(block, block, s_sib.at[k], sibling)

    def relay_a(k):
        if k % 2 == 0:
            one = shards(qs[k], last, f_minus)
            send(one, one, s_a.at[k, 2], on_a(1))
        else:
            one = shards(qs[k], last, f_plus)
            send(one, one, s_a.at[k, 2], on_a(3))

    def arrive_a(k):
        wait(shards(qs[k], last, f_minus), s_a.at[k, 0])
        if k % 2 == 0:
            relay_a(k)
        if k == 0:
            send_b_one(f_minus)
        wait(shards(qs[k], last, f_plus), s_a.at[k, 1])
        if k % 2 == 1:
            relay_a(k)
        if k == 0:
            send_b_one(f_plus)

    def finish_a(k):
        wait(shards(qs[k], last, f_far), s_a.at[k, 2])
        if k == 0:
            send_b_one(f_far)
        else:
            block = shards(qs[k], last, 0, 4)
            send(block, block, s_b.at[k, 0], on_b(1))
            send(block, block, s_b.at[k, 1], on_b(3))
        send_sib(k, last)

    def arrive_b(k):
        wait(shards(qs[k], l_minus, 0, 4), s_b.at[k, 0])
        half = shards(qs[k], l_minus, 0, 2)
        send(half, half, s_b.at[k, 2], on_b(1))
        wait(shards(qs[k], l_plus, 0, 4), s_b.at[k, 1])
        half = shards(qs[k], l_plus, 2, 2)
        send(half, half, s_b.at[k, 3], on_b(3))
        send_sib(k, l_minus)
        send_sib(k, l_plus)

    def finish_b(k):
        wait(shards(qs[k], l_far, 0, 2), s_b.at[k, 2])
        wait(shards(qs[k], l_far, 2, 2), s_b.at[k, 3])
        send_sib(k, l_far)

    def part_at(mine, k, i=0, count=4):
        return pl.ds(((0 if mine else 4) + k) * 4 + i, count)

    def multiply(mine, k):
        p = c if mine else 1 - c
        base = (p * 4 + qs[k]) * 16
        rows = [tok[base + i * (4 - 3 * p) + j * (1 + 3 * p)] for i in range(4) for j in range(4)]
        lhs = jnp.concatenate(rows, axis=0)
        for n in range(2):
            prod = jnp.dot(lhs, wts[:, n * 256 : (n + 1) * 256], preferred_element_type=jnp.float32)
            for i in range(4):
                scaled = prod[i * 64 : (i + 1) * 64] * coef[2 * i + p, src]
                part[((0 if mine else 4) + k) * 4 + i, :, :, n * 256 : (n + 1) * 256] = scaled.reshape(4, 16, 256)

    def own_rows(k):
        multiply(True, k)

    def sibling_rows(k):
        wait(tok.at[pl.ds((1 - c) * 64 + qs[k] * 16, 16)], s_sib.at[k])
        multiply(False, k)
        ref = part.at[part_at(False, k)]
        send(ref, r_sib.at[k], s_rsib.at[k], sibling, 1)

    def reduce_a(k):
        wait(r_sib.at[k], s_rsib.at[k])
        away, here = 2 * (1 - row), 2 * row
        at = part_at(True, k)
        z_out[k] = part[at, pl.ds(away, 2)] + r_sib[k, :, pl.ds(away, 2)]
        send(z_out.at[k], r_z.at[k], s_rz.at[k], partner, 1)
        part[at, pl.ds(here, 2)] = part[at, pl.ds(here, 2)] + r_sib[k, :, pl.ds(here, 2)]

    y_minus, y_plus, y_far = mod4(y + 3), mod4(y + 1), mod4(y + 2)

    def reduce_b(k):
        wait(r_z.at[k], s_rz.at[k])
        at = part_at(True, k)
        part[at, pl.ds(2 * row, 2)] = part[at, pl.ds(2 * row, 2)] + r_z[k]
        send(part.at[k * 4 + y_far, 2 * row], r_y2.at[k, 0], s_ry2.at[k, 0], device(dy=1), 1)
        send(part.at[k * 4 + y_far, 2 * row + 1], r_y2.at[k, 1], s_ry2.at[k, 1], device(dy=3), 1)

    def reduce_c(k):
        wait(r_y2.at[k, 0], s_ry2.at[k, 0])
        part[k * 4 + y_plus, 2 * row] = part[k * 4 + y_plus, 2 * row] + r_y2[k, 0]
        send(part.at[k * 4 + y_plus, pl.ds(2 * row, 2)], r_y1.at[k, 0], s_ry1.at[k, 0], device(dy=1), 1)
        wait(r_y2.at[k, 1], s_ry2.at[k, 1])
        part[k * 4 + y_minus, 2 * row + 1] = part[k * 4 + y_minus, 2 * row + 1] + r_y2[k, 1]
        send(part.at[k * 4 + y_minus, pl.ds(2 * row, 2)], r_y1.at[k, 1], s_ry1.at[k, 1], device(dy=3), 1)

    def reduce_d(k):
        wait(r_y1.at[k, 0], s_ry1.at[k, 0])
        wait(r_y1.at[k, 1], s_ry1.at[k, 1])
        for a in range(2):
            total = part[k * 4 + y, 2 * row + a] + r_y1[k, 0, a] + r_y1[k, 1, a]
            gate, up = total[:, :256], total[:, 256:]
            out_ref[a, qs[k]] = (gate / (1.0 + jnp.exp(-gate)) * up).astype(jnp.bfloat16)

    one = shards(zh, last, first)
    send(one, one, s_z.at[0], device(dz=1))
    send(one, one, s_z.at[1], device(dz=3))
    send_a(0)
    send_b_one(first)
    send(one, one, s_z.at[2], device(dz=2))
    arrive_a(0)
    wait(shards(qs[1], last, first), s_z.at[0])
    send_a(1)
    wait(shards(qs[2], last, first), s_z.at[1])
    send_a(2)
    finish_a(0)
    arrive_a(1)
    finish_a(1)
    wait(shards(qs[3], last, first), s_z.at[2])
    send_a(3)
    gate_in.wait()
    up_in.wait()

    arrive_b(0)
    arrive_a(2)
    finish_a(2)
    finish_b(0)
    own_rows(0)
    arrive_b(1)
    arrive_a(3)
    finish_a(3)
    sibling_rows(0)
    finish_b(1)
    own_rows(1)
    reduce_a(0)
    arrive_b(2)
    sibling_rows(1)
    reduce_b(0)
    finish_b(2)
    own_rows(2)
    arrive_b(3)
    reduce_a(1)
    reduce_c(0)
    sibling_rows(2)
    reduce_b(1)
    reduce_d(0)
    finish_b(3)
    own_rows(3)
    reduce_a(2)
    reduce_c(1)
    sibling_rows(3)
    reduce_b(2)
    reduce_d(1)
    reduce_a(3)
    reduce_c(2)
    reduce_b(3)
    reduce_d(2)
    reduce_c(3)
    reduce_d(3)
    wait(tok.at[pl.ds(0, 127)], s_send.at[0])
    wait(part.at[pl.ds(0, 30)], s_send.at[1])


def shards_fn(tokens, coefficients, gate_weights, up_weights):
    dma = pltpu.SemaphoreType.DMA
    hidden = pl.pallas_call(
        kernel,
        out_shape=jax.ShapeDtypeStruct((2, 4, 16, 256), jnp.bfloat16),
        in_specs=[
            pl.BlockSpec(memory_space=pl.ANY),
            pl.BlockSpec(memory_space=pltpu.SMEM),
            pl.BlockSpec(memory_space=pl.ANY),
            pl.BlockSpec(memory_space=pl.ANY),
        ],
        out_specs=pl.BlockSpec(memory_space=pltpu.VMEM),
        scratch_shapes=[
            pltpu.VMEM((128, 16, 4096), jnp.bfloat16),
            pltpu.VMEM((4096, 512), jnp.bfloat16),
            pltpu.VMEM((32, 4, 16, 512), jnp.float32),
            pltpu.VMEM((4, 4, 4, 16, 512), jnp.float32),
            pltpu.VMEM((4, 4, 2, 16, 512), jnp.float32),
            pltpu.VMEM((4, 4, 2, 16, 512), jnp.float32),
            pltpu.VMEM((4, 2, 16, 512), jnp.float32),
            pltpu.VMEM((4, 2, 2, 16, 512), jnp.float32),
            dma((3,)), dma((2,)), dma((3,)), dma((4, 3)), dma((4, 4)), dma((1,)),
            dma((4,)), dma((4,)), dma((4,)), dma((4, 2)), dma((4, 2)),
        ],
        compiler_params=pltpu.CompilerParams(collective_id=0, has_side_effects=True, vmem_limit_bytes=60 * 1024 * 1024),
    )(tokens, coefficients, gate_weights, up_weights)
    return hidden.reshape(1, 128, 256)


def solution(mesh):
    return jax.shard_map(
        shards_fn,
        mesh=mesh,
        in_specs=(P("src", "tp", "row"), P(), P("src", "row", "tp"), P("src", "row", "tp")),
        out_specs=P("src", "row", "tp"),
        check_vma=False,
    )
```

time: 212 us -> 91.1 us (0.43)
  the two profiles are of different devices: /device:TPU:1 before, /device:TPU:164 now
where the time goes in v1:
time: 91.1 us; the launch traced here: 91 us
  Pallas kernels  89.5 us (98%)
  local copies, waits for them, and re-layouts  1.47 us (2%)
    pallas_call x1, Pallas kernels, shards_fn(): pl.pallas_call(kernel, out_shape=jax.ShapeDtypeStruct((2, 4, 16, 256), jn...  89.5 us

profile of v1, /device:TPU:164, one launch (start us, length us, event | category | flops | bytes accessed | tf_op | source)
XLA Modules:
  0.0 91.0 jit_solution(8413467170524431672)
XLA Ops:
  0.0 89.5 %shard_map.46 = bf16[2,4,16,256]{3,2,1,0:T(8,128)(2,1)} custom-call(bf16[1,16,4096]{2,1,0:T(8,128)(2,1)} %tok_hbm.1, f32[8,8]{1,0:T(8,128)} %coef.1, bf16[1,4096,256]{2,1,0:T(8,128)(2,1)} %gate_hbm.1, bf16[1,4096,256]{2,1,0:T(8,128)(2,1)} %up_hbm.1), custom_call_target="tpu_custom_call" | custom-call | tf_op jit(solution)/shard_map/pallas_call | solution.py:247
  89.5 1.5 %copy.6 = bf16[1,128,256]{2,1,0:T(8,128)(2,1)} copy(bf16[1,128,256]{2,1,0:T(8,128)(2,1)} %bitcast.1) | data formatting | bytes 131072

commit v2 on v0

v2 whole, which is shorter than its diff:
```python
import jax
import jax.numpy as jnp
from jax import lax
from jax.experimental import pallas as pl
from jax.experimental.pallas import tpu as pltpu
from jax.sharding import PartitionSpec as P

MESH = pl.DeviceIdType.MESH


def mod4(value):
    return lax.rem(value, jnp.int32(4))


def kernel(
    tok_hbm, coef, gate_hbm, up_hbm, out_ref,
    tok, wts, part, r_sib, z_out, r_z, r_y,
    s_local, s_send, s_z, s_a, s_b, s_f, s_sib, s_rsib, s_rz, s_ry,
):
    src, tp, row = lax.axis_index("src"), lax.axis_index("tp"), lax.axis_index("row")
    y, c = lax.div(src, jnp.int32(2)), lax.rem(src, jnp.int32(2))
    x, zh = lax.div(tp, jnp.int32(4)), mod4(tp)

    first = x * (1 - c) + y * c

    def last(core):
        return y * (1 - core) + x * core

    def device(dx=0, dy=0, dz=0):
        return (2 * mod4(y + dy) + c, 4 * mod4(x + dx) + mod4(zh + dz), row)

    def on_a(step):
        return device(dx=step * (1 - c), dy=step * c)

    def on_b(step):
        return device(dx=step * c, dy=step * (1 - c))

    sibling = (2 * y + 1 - c, tp, row)
    partner = (src, tp, 1 - row)
    qs = [mod4(zh + d) for d in (0, 3, 1, 2)]
    fs = [mod4(first + d) for d in (0, 3, 1, 2)]

    def shards(k, dl, f=0, count=1):
        return tok.at[pl.ds(((c * 4 + qs[k]) * 4 + mod4(last(c) + dl)) * 4 + f, count)]

    def send(ref, there, sem, to, kind=0):
        pltpu.make_async_remote_copy(
            src_ref=ref, dst_ref=there, send_sem=s_send.at[kind], recv_sem=sem, device_id=to, device_id_type=MESH
        ).start()

    def wait(ref, sem):
        pltpu.make_async_copy(ref, ref, sem).wait()

    own = pltpu.make_async_copy(tok_hbm, shards(0, 0, fs[0]), s_local.at[0])
    gate_in = pltpu.make_async_copy(gate_hbm.at[0], wts.at[:, pl.ds(0, 256)], s_local.at[1])
    up_in = pltpu.make_async_copy(up_hbm.at[0], wts.at[:, pl.ds(256, 256)], s_local.at[2])
    own.start()
    gate_in.start()
    up_in.start()

    barrier = pltpu.get_barrier_semaphore()
    greeted = [device(dx=1), device(dx=3), device(dy=1), device(dy=3), device(dy=2)]
    greeted += [device(dz=1), device(dz=3), device(dz=2), sibling, partner]
    for one in greeted:
        pl.semaphore_signal(barrier, inc=1, device_id=one, device_id_type=MESH)
    own.wait()
    pl.semaphore_wait(barrier, len(greeted))

    def send_b(k, j):
        one = shards(k, 0, fs[j])
        send(one, one, s_b.at[k, 0, j // 2], on_b(1))
        send(one, one, s_b.at[k, 1, j // 2], on_b(3))

    def send_a(k):
        one = shards(k, 0, fs[0])
        send(one, one, s_a.at[k, 0], on_a(1))
        send(one, one, s_a.at[k, 1], on_a(3))

    def relay_a(k):
        one = shards(k, 0, fs[1 + k % 2])
        send(one, one, s_a.at[k, 2], on_a(1 + 2 * (k % 2)))

    def sib(k, dl):
        block = shards(k, dl, 0, 4)
        send(block, block, s_sib.at[k, int(dl == 2)], sibling)

    def start():
        one = shards(0, 0, fs[0])
        send(one, one, s_z.at[0], device(dz=1))
        send(one, one, s_z.at[1], device(dz=3))
        send_a(0)
        send_b(0, 0)
        send(one, one, s_z.at[2], device(dz=2))

    def z(k):
        wait(shards(k, 0, fs[0]), s_z.at[k - 1])
        send_a(k)
        send_b(k, 0)

    def a(k, j):
        wait(shards(k, 0, fs[j]), s_a.at[k, j - 1])
        if j == 1 + k % 2:
            relay_a(k)
        send_b(k, j)
        if j == 3:
            sib(k, 0)

    def b1(k):
        wait(shards(k, 3, 0, 2), s_b.at[k, 0, 0])
        for j in (0, 1):
            one = shards(k, 3, fs[j])
            send(one, one, s_f.at[k, 0], on_b(1))

    def b2(k):
        wait(shards(k, 1, 0, 2), s_b.at[k, 1, 1])
        for j in (2, 3):
            one = shards(k, 1, fs[j])
            send(one, one, s_f.at[k, 1], on_b(3))

    def sib_near(k):
        wait(shards(k, 1, 0, 2), s_b.at[k, 1, 0])
        sib(k, 1)
        wait(shards(k, 3, 0, 2), s_b.at[k, 0, 1])
        sib(k, 3)

    def b3(k):
        wait(shards(k, 2, 0, 2), s_f.at[k, 0])
        wait(shards(k, 2, 0, 2), s_f.at[k, 1])
        sib(k, 2)

    def blocks(portion):
        return (2,) if portion[1] else (0, 1, 3)

    def multiply(mine, portions):
        p = c if mine else 1 - c
        pairs = [(portion[0], mod4(last(p) + d)) for portion in portions for d in blocks(portion)]
        lhs = jnp.concatenate([tok[(p * 4 + qs[k]) * 16 + l * 4 + f] for k, l in pairs for f in range(4)], axis=0)
        for n in range(2):
            prod = jnp.dot(lhs, wts[:, n * 256 : (n + 1) * 256], preferred_element_type=jnp.float32)
            for i, (k, l) in enumerate(pairs):
                for f in range(4):
                    at = (i * 4 + f) * 16
                    scaled = prod[at : at + 16] * coef[2 * (l * (1 - p) + f * p) + p, src]
                    part[((0 if mine else 4) + k) * 4 + l, f, :, n * 256 : (n + 1) * 256] = scaled

    def own_rows(*portions):
        multiply(True, portions)

    def sibling_rows(*portions):
        for portion in portions:
            wait(tok.at[pl.ds(0, 4 * len(blocks(portion)))], s_sib.at[portion])
        multiply(False, portions)
        for portion in portions:
            for d in blocks(portion):
                l = portion[0] * 4 + mod4(last(1 - c) + d)
                send(part.at[16 + l], r_sib.at[l], s_rsib.at[portion], sibling, 1)

    here, away = 2 * row, 2 * (1 - row)

    def reduce_1(k, late):
        wait(r_sib.at[pl.ds(0, len(blocks((k, late))))], s_rsib.at[k, late])

        @pl.when(c == 0)
        def _():
            for d in blocks((k, late)):
                l = k * 4 + mod4(y + d)
                out, there = z_out.at[k, d, pl.ds(0, 2)], r_z.at[k, d, pl.ds(0, 2)]
                out[...] = part[l, pl.ds(away, 2)] + r_sib[l, pl.ds(away, 2)]
                send(out, there, s_rz.at[k, d], partner, 1)
                part[l, pl.ds(here, 2)] = part[l, pl.ds(here, 2)] + r_sib[l, pl.ds(here, 2)]

        @pl.when(c == 1)
        def _():
            for d in blocks((k, late)):
                l = mod4(x + d)

                @pl.when(lax.div(l, jnp.int32(2)) != row)
                def _():
                    z_out[k, d] = part[k * 4 + l] + r_sib[k * 4 + l]
                    send(z_out.at[k, d], r_z.at[k, d], s_rz.at[k, d], partner, 1)

                @pl.when(lax.div(l, jnp.int32(2)) == row)
                def _():
                    part[k * 4 + l] = part[k * 4 + l] + r_sib[k * 4 + l]

    def reduce_2(k, late):
        @pl.when(c == 0)
        def _():
            for d in blocks((k, late)):
                l = k * 4 + mod4(y + d)
                wait(r_z.at[k, d, pl.ds(0, 2)], s_rz.at[k, d])
                part[l, pl.ds(here, 2)] = part[l, pl.ds(here, 2)] + r_z[k, d, pl.ds(0, 2)]
                if d:
                    send(part.at[l, pl.ds(here, 2)], r_y.at[k, d - 1], s_ry.at[k, d - 1, 0], device(dy=d), 1)

        @pl.when(c == 1)
        def _():
            for d in blocks((k, late)):
                l = mod4(x + d)

                @pl.when(lax.div(l, jnp.int32(2)) == row)
                def _():
                    wait(r_z.at[k, d], s_rz.at[k, d])
                    part[k * 4 + l] = part[k * 4 + l] + r_z[k, d]
                    odd = lax.rem(l, jnp.int32(2))
                    for e in (2, 1, 3):
                        spot = part.at[k * 4 + l, mod4(y + e)]
                        send(spot, r_y.at[k, e - 1, odd], s_ry.at[k, e - 1, odd], device(dy=e), 1)

    def finish(k, a, mine):
        total = mine + r_y[k, 0, a] + r_y[k, 1, a] + r_y[k, 2, a]
        gate, up = total[:, :256], total[:, 256:]
        out_ref[a, qs[k]] = (gate / (1.0 + jnp.exp(-gate)) * up).astype(jnp.bfloat16)

    def reduce_3(k):
        @pl.when(c == 0)
        def _():
            for i in (0, 2, 1):
                wait(r_y.at[k, i], s_ry.at[k, i, 0])
            for a in range(2):
                finish(k, a, part[k * 4 + y, here + a])

        @pl.when(c == 1)
        def _():
            for i in (0, 2, 1):
                for a in range(2):
                    wait(r_y.at[k, i, a], s_ry.at[k, i, a])
            for a in range(2):
                finish(k, a, part[k * 4 + here + a, y])

    start()
    a(0,1)
    a(0,2)
    a(0,3)
    z(1)
    z(2)
    b1(0)
    a(1,1)
    a(1,2)
    a(2,1)
    a(2,2)
    b2(0)
    sib_near(0)
    gate_in.wait()
    up_in.wait()
    own_rows((0,0))
    a(1,3)
    z(3)
    a(2,3)
    b1(1)
    sibling_rows((0,0))
    a(3,1)
    a(3,2)
    reduce_1(0,0)
    b2(1)
    a(3,3)
    b3(0)
    sib_near(1)
    own_rows((1,0),(0,1))
    b1(2)
    b2(2)
    b1(3)
    sibling_rows((1,0),(0,1))
    sib_near(2)
    reduce_2(0,0)
    b3(1)
    reduce_1(0,1)
    reduce_1(1,0)
    own_rows((2,0),(1,1))
    b2(3)
    sib_near(3)
    sibling_rows((2,0),(1,1))
    reduce_2(0,1)
    reduce_2(1,0)
    reduce_1(1,1)
    reduce_1(2,0)
    b3(2)
    own_rows((3,0),(2,1))
    sibling_rows((3,0),(2,1))
    reduce_3(0)
    reduce_2(1,1)
    b3(3)
    own_rows((3,1))
    reduce_1(2,1)
    reduce_1(3,0)
    reduce_2(2,0)
    sibling_rows((3,1))
    reduce_3(1)
    reduce_2(2,1)
    reduce_1(3,1)
    reduce_2(3,0)
    reduce_3(2)
    reduce_2(3,1)
    reduce_3(3)
    wait(tok.at[pl.ds(0, 127)], s_send.at[0])
    wait(part.at[pl.ds(0, 30)], s_send.at[1])


def shards_fn(tokens, coefficients, gate_weights, up_weights):
    dma = pltpu.SemaphoreType.DMA
    hidden = pl.pallas_call(
        kernel,
        out_shape=jax.ShapeDtypeStruct((2, 4, 16, 256), jnp.bfloat16),
        in_specs=[
            pl.BlockSpec(memory_space=pl.ANY),
            pl.BlockSpec(memory_space=pltpu.SMEM),
            pl.BlockSpec(memory_space=pl.ANY),
            pl.BlockSpec(memory_space=pl.ANY),
        ],
        out_specs=pl.BlockSpec(memory_space=pltpu.VMEM),
        scratch_shapes=[
            pltpu.VMEM((128, 16, 4096), jnp.bfloat16),
            pltpu.VMEM((4096, 512), jnp.bfloat16),
            pltpu.VMEM((32, 4, 16, 512), jnp.float32),
            pltpu.VMEM((16, 4, 16, 512), jnp.float32),
            pltpu.VMEM((4, 4, 4, 16, 512), jnp.float32),
            pltpu.VMEM((4, 4, 4, 16, 512), jnp.float32),
            pltpu.VMEM((4, 3, 2, 16, 512), jnp.float32),
            dma((3,)), dma((2,)), dma((3,)), dma((4, 3)), dma((4, 2, 2)), dma((4, 2)),
            dma((4, 2)), dma((4, 2)), dma((4, 4)), dma((4, 3, 2)),
        ],
        compiler_params=pltpu.CompilerParams(collective_id=0, has_side_effects=True, vmem_limit_bytes=60 * 1024 * 1024),
    )(tokens, coefficients, gate_weights, up_weights)
    return hidden.reshape(1, 128, 256)


def solution(mesh):
    return jax.shard_map(
        shards_fn,
        mesh=mesh,
        in_specs=(P("src", "tp", "row"), P(), P("src", "row", "tp"), P("src", "row", "tp")),
        out_specs=P("src", "row", "tp"),
        check_vma=False,
    )
```

time: 212 us -> 79.8 us (0.38)
  the two profiles are of different devices: /device:TPU:1 before, /device:TPU:6 now
where the time goes in v2:
time: 79.8 us; the launch traced here: 79.6 us
  Pallas kernels  78.1 us (98%)
  local copies, waits for them, and re-layouts  1.47 us (2%)
    pallas_call x1, Pallas kernels, shards_fn(): pl.pallas_call(kernel, out_shape=jax.ShapeDtypeStruct((2, 4, 16, 256), jn...  78.1 us

profile of v2, /device:TPU:6, one launch (start us, length us, event | category | flops | bytes accessed | tf_op | source)
XLA Modules:
  0.0 79.6 jit_solution(9051300045462563184)
XLA Ops:
  0.0 78.1 %shard_map.46 = bf16[2,4,16,256]{3,2,1,0:T(8,128)(2,1)} custom-call(bf16[1,16,4096]{2,1,0:T(8,128)(2,1)} %tok_hbm.1, f32[8,8]{1,0:T(8,128)} %coef.1, bf16[1,4096,256]{2,1,0:T(8,128)(2,1)} %gate_hbm.1, bf16[1,4096,256]{2,1,0:T(8,128)(2,1)} %up_hbm.1), custom_call_target="tpu_custom_call" | custom-call | tf_op jit(solution)/shard_map/pallas_call | solution.py:301
  78.1 1.5 %copy.6 = bf16[1,128,256]{2,1,0:T(8,128)(2,1)} copy(bf16[1,128,256]{2,1,0:T(8,128)(2,1)} %bitcast.1) | data formatting | bytes 131072

commit v3 on v2

--- a/solution.py
+++ b/solution.py
@@ -14,8 +14,8 @@
 
 def kernel(
     tok_hbm, coef, gate_hbm, up_hbm, out_ref,
-    tok, wts, part, r_sib, z_out, r_z, r_y,
-    s_local, s_send, s_z, s_a, s_b, s_f, s_sib, s_rsib, s_rz, s_ry,
+    tok, wts, part, r_sib, z_out, r_z, r_y, r_w,
+    s_local, s_send, s_z, s_a, s_b, s_f, s_sib, s_rsib, s_rz, s_ry, s_w,
 ):
     src, tp, row = lax.axis_index("src"), lax.axis_index("tp"), lax.axis_index("row")
     y, c = lax.div(src, jnp.int32(2)), lax.rem(src, jnp.int32(2))
@@ -84,26 +84,46 @@
         block = shards(k, dl, 0, 4)
         send(block, block, s_sib.at[k, int(dl == 2)], sibling)
 
+    def send_z(j):
+        one = shards(0, 0, fs[j])
+        send(one, one, s_z.at[1, j // 2], device(dz=1))
+        send(one, one, s_z.at[2, j // 2], device(dz=3))
+
     def start():
-        one = shards(0, 0, fs[0])
-        send(one, one, s_z.at[0], device(dz=1))
-        send(one, one, s_z.at[1], device(dz=3))
+        send_z(0)
         send_a(0)
         send_b(0, 0)
-        send(one, one, s_z.at[2], device(dz=2))
+
+        @pl.when(c == 0)
+        def _():
+            one = shards(0, 0, fs[0])
+            send(one, one, s_z.at[3, 0], device(dz=2))
 
     def z(k):
-        wait(shards(k, 0, fs[0]), s_z.at[k - 1])
+        wait(shards(k, 0, fs[0]), s_z.at[k, 0])
         send_a(k)
-        send_b(k, 0)
 
     def a(k, j):
         wait(shards(k, 0, fs[j]), s_a.at[k, j - 1])
         if j == 1 + k % 2:
             relay_a(k)
-        send_b(k, j)
-        if j == 3:
-            sib(k, 0)
+        if k == 0:
+            send_b(0, j)
+
+            @pl.when(c == 1)
+            def _():
+                send_z(j)
+
+    def zc(k, half):
+        wait(shards(k, 0, 0, 2), s_z.at[k, half])
+        if k == half + 1:
+            for i in (2 * half, 2 * half + 1):
+                one = shards(k, 0, fs[i])
+                send(one, one, s_z.at[3, half], device(dz=1 + 2 * half))
+
+    def o(k, half):
+        send_b(k, 2 * half)
+        send_b(k, 2 * half + 1)
 
     def b1(k):
         wait(shards(k, 3, 0, 2), s_b.at[k, 0, 0])
@@ -207,10 +227,12 @@
                         spot = part.at[k * 4 + l, mod4(y + e)]
                         send(spot, r_y.at[k, e - 1, odd], s_ry.at[k, e - 1, odd], device(dy=e), 1)
 
-    def finish(k, a, mine):
-        total = mine + r_y[k, 0, a] + r_y[k, 1, a] + r_y[k, 2, a]
+    def activate(k, a, total):
         gate, up = total[:, :256], total[:, 256:]
         out_ref[a, qs[k]] = (gate / (1.0 + jnp.exp(-gate)) * up).astype(jnp.bfloat16)
+
+    def finish(k, a, mine):
+        activate(k, a, mine + r_y[k, 0, a] + r_y[k, 1, a] + r_y[k, 2, a])
 
     def reduce_3(k):
         @pl.when(c == 0)
@@ -228,70 +250,198 @@
             for a in range(2):
                 finish(k, a, part[k * 4 + here + a, y])
 
+    def last_1(late):
+        wait(r_sib.at[pl.ds(0, len(blocks((3, late))))], s_rsib.at[3, late])
+        for d in blocks((3, late)):
+            l = mod4(x + d)
+            part[12 + l] = part[12 + l] + r_sib[12 + l]
+            for e in (2, 1, 3):
+                send(part.at[12 + l, mod4(y + e)], r_w.at[e - 1, l], s_w.at[e - 1, l], device(dy=e), 1)
+
+    def last_2():
+        for i in (0, 2, 1):
+            for l in range(4):
+                wait(r_w.at[i, l], s_w.at[i, l])
+
+        def total(l):
+            return part[12 + l, y] + r_w[0, l] + r_w[1, l] + r_w[2, l]
+
+        for i in range(2):
+            z_out[3, 0, i] = total(away + i)
+        send(z_out.at[3, 0, pl.ds(0, 2)], r_z.at[3, 0, pl.ds(0, 2)], s_rz.at[3, 0], partner, 1)
+        for i in range(2):
+            z_out[3, 1, i] = total(here + i)
+
+    def last_3():
+        wait(r_z.at[3, 0, pl.ds(0, 2)], s_rz.at[3, 0])
+        for i in range(2):
+            activate(3, i, z_out[3, 1, i] + r_z[3, 0, i])
+
     start()
     a(0,1)
     a(0,2)
     a(0,3)
-    z(1)
-    z(2)
+    sib(0,0)
+    @pl.when(c == 0)
+    def _():
+        z(1)
+
+    @pl.when(c == 0)
+    def _():
+        z(2)
+
     b1(0)
-    a(1,1)
-    a(1,2)
-    a(2,1)
-    a(2,2)
+    @pl.when(c == 0)
+    def _():
+        a(1,1)
+
+    @pl.when(c == 1)
+    def _():
+        zc(1,0)
+
+    o(1,0)
+    @pl.when(c == 0)
+    def _():
+        a(1,2)
+
+    @pl.when(c == 0)
+    def _():
+        a(2,1)
+
+    @pl.when(c == 0)
+    def _():
+        a(2,2)
+
+    @pl.when(c == 1)
+    def _():
+        zc(2,0)
+
     b2(0)
     sib_near(0)
     gate_in.wait()
     up_in.wait()
     own_rows((0,0))
-    a(1,3)
-    z(3)
-    a(2,3)
+    @pl.when(c == 0)
+    def _():
+        a(1,3)
+
+    @pl.when(c == 1)
+    def _():
+        zc(1,1)
+
+    o(1,1)
+    sib(1,0)
+    @pl.when(c == 0)
+    def _():
+        z(3)
+
+    @pl.when(c == 1)
+    def _():
+        zc(2,1)
+
+    sibling_rows((0,0))
     b1(1)
-    sibling_rows((0,0))
-    a(3,1)
-    a(3,2)
+    @pl.when(c == 0)
+    def _():
+        a(2,3)
+
+    o(2,0)
+    sib(2,0)
+    b3(0)
+    @pl.when(c == 0)
+    def _():
+        a(3,1)
+
+    @pl.when(c == 0)
+    def _():
+        a(3,2)
+
+    b2(1)
+    o(2,1)
     reduce_1(0,0)
-    b2(1)
-    a(3,3)
-    b3(0)
     sib_near(1)
+    @pl.when(c == 1)
+    def _():
+        zc(3,0)
+
+    o(3,0)
     own_rows((1,0),(0,1))
+    sibling_rows((1,0),(0,1))
     b1(2)
-    b2(2)
-    b1(3)
-    sibling_rows((1,0),(0,1))
-    sib_near(2)
+    @pl.when(c == 0)
+    def _():
+        a(3,3)
+
+    @pl.when(c == 1)
+    def _():
+        zc(3,1)
+
+    o(3,1)
+    sib(3,0)
     reduce_2(0,0)
-    b3(1)
     reduce_1(0,1)
     reduce_1(1,0)
+    b2(2)
+    sib_near(2)
+    b3(1)
     own_rows((2,0),(1,1))
-    b2(3)
-    sib_near(3)
+    b1(3)
     sibling_rows((2,0),(1,1))
     reduce_2(0,1)
+    b2(3)
     reduce_2(1,0)
     reduce_1(1,1)
     reduce_1(2,0)
+    sib_near(3)
     b3(2)
     own_rows((3,0),(2,1))
     sibling_rows((3,0),(2,1))
-    reduce_3(0)
     reduce_2(1,1)
     b3(3)
     own_rows((3,1))
+    @pl.when(c == 0)
+    def _():
+        reduce_1(3,0)
+
+    @pl.when(c == 1)
+    def _():
+        last_1(0)
+
     reduce_1(2,1)
-    reduce_1(3,0)
     reduce_2(2,0)
     sibling_rows((3,1))
+    reduce_3(0)
+    @pl.when(c == 0)
+    def _():
+        reduce_1(3,1)
+
+    @pl.when(c == 1)
+    def _():
+        last_1(1)
+
+    reduce_2(2,1)
     reduce_3(1)
-    reduce_2(2,1)
-    reduce_1(3,1)
-    reduce_2(3,0)
+    @pl.when(c == 0)
+    def _():
+        reduce_2(3,0)
+
+    @pl.when(c == 0)
+    def _():
+        reduce_2(3,1)
+
+    @pl.when(c == 1)
+    def _():
+        last_2()
+
     reduce_3(2)
-    reduce_2(3,1)
-    reduce_3(3)
+    @pl.when(c == 0)
+    def _():
+        reduce_3(3)
+
+    @pl.when(c == 1)
+    def _():
+        last_3()
+
     wait(tok.at[pl.ds(0, 127)], s_send.at[0])
     wait(part.at[pl.ds(0, 30)], s_send.at[1])
 
@@ -316,8 +466,9 @@
             pltpu.VMEM((4, 4, 4, 16, 512), jnp.float32),
             pltpu.VMEM((4, 4, 4, 16, 512), jnp.float32),
             pltpu.VMEM((4, 3, 2, 16, 512), jnp.float32),
-            dma((3,)), dma((2,)), dma((3,)), dma((4, 3)), dma((4, 2, 2)), dma((4, 2)),
-            dma((4, 2)), dma((4, 2)), dma((4, 4)), dma((4, 3, 2)),
+            pltpu.VMEM((3, 4, 16, 512), jnp.float32),
+            dma((3,)), dma((2,)), dma((4, 2)), dma((4, 3)), dma((4, 2, 2)), dma((4, 2)),
+            dma((4, 2)), dma((4, 2)), dma((4, 4)), dma((4, 3, 2)), dma((3, 4)),
         ],
         compiler_params=pltpu.CompilerParams(collective_id=0, has_side_effects=True, vmem_limit_bytes=60 * 1024 * 1024),
     )(tokens, coefficients, gate_weights, up_weights)

time: 79.8 us -> 76.9 us (0.964)
  the two profiles are of different devices: /device:TPU:6 before, /device:TPU:1 now
where the time goes in v3:
time: 76.9 us; the launch traced here: 75.9 us
  Pallas kernels  74.4 us (97%)
  local copies, waits for them, and re-layouts  1.47 us (2%)
    pallas_call x1, Pallas kernels, shards_fn(): pl.pallas_call(kernel, out_shape=jax.ShapeDtypeStruct((2, 4, 16, 256), jn...  74.4 us

profile of v3, /device:TPU:1, one launch (start us, length us, event | category | flops | bytes accessed | tf_op | source)
XLA Modules:
  0.0 75.9 jit_solution(16760850304943968003)
XLA Ops:
  0.0 74.4 %shard_map.46 = bf16[2,4,16,256]{3,2,1,0:T(8,128)(2,1)} custom-call(bf16[1,16,4096]{2,1,0:T(8,128)(2,1)} %tok_hbm.1, f32[8,8]{1,0:T(8,128)} %coef.1, bf16[1,4096,256]{2,1,0:T(8,128)(2,1)} %gate_hbm.1, bf16[1,4096,256]{2,1,0:T(8,128)(2,1)} %up_hbm.1), custom_call_target="tpu_custom_call" | custom-call | tf_op jit(solution)/shard_map/pallas_call | solution.py:451
  74.4 1.5 %copy.6 = bf16[1,128,256]{2,1,0:T(8,128)(2,1)} copy(bf16[1,128,256]{2,1,0:T(8,128)(2,1)} %bitcast.1) | data formatting | bytes 131072

commit v4 on v3

--- a/solution.py
+++ b/solution.py
@@ -282,6 +282,7 @@
     a(0,2)
     a(0,3)
     sib(0,0)
+    b1(0)
     @pl.when(c == 0)
     def _():
         z(1)
@@ -290,7 +291,7 @@
     def _():
         z(2)
 
-    b1(0)
+    b2(0)
     @pl.when(c == 0)
     def _():
         a(1,1)
@@ -316,7 +317,6 @@
     def _():
         zc(2,0)
 
-    b2(0)
     sib_near(0)
     gate_in.wait()
     up_in.wait()
@@ -378,7 +378,6 @@
 
     o(3,1)
     sib(3,0)
-    reduce_2(0,0)
     reduce_1(0,1)
     reduce_1(1,0)
     b2(2)
@@ -387,27 +386,28 @@
     own_rows((2,0),(1,1))
     b1(3)
     sibling_rows((2,0),(1,1))
-    reduce_2(0,1)
     b2(3)
-    reduce_2(1,0)
     reduce_1(1,1)
     reduce_1(2,0)
     sib_near(3)
+    reduce_2(0,0)
+    reduce_2(0,1)
+    reduce_2(1,0)
     b3(2)
     own_rows((3,0),(2,1))
     sibling_rows((3,0),(2,1))
     reduce_2(1,1)
     b3(3)
     own_rows((3,1))
+    @pl.when(c == 1)
+    def _():
+        last_1(0)
+
+    reduce_1(2,1)
     @pl.when(c == 0)
     def _():
         reduce_1(3,0)
 
-    @pl.when(c == 1)
-    def _():
-        last_1(0)
-
-    reduce_1(2,1)
     reduce_2(2,0)
     sibling_rows((3,1))
     reduce_3(0)

time: 76.9 us -> 74.9 us (0.974); the launches traced: 75.9 us -> 74.8 us
  Pallas kernels: 74.4 us -> 73.3 us
    pallas_call x1, Pallas kernels: 74.4 us -> 73.3 us  [shards_fn(): pl.pallas_call(kernel, out_shape=jax.ShapeDtypeStruct((2, 4, 16, 256), jn...]
where the time goes in v4:
time: 74.9 us; the launch traced here: 74.8 us
  Pallas kernels  73.3 us (98%)
  local copies, waits for them, and re-layouts  1.47 us (2%)
    pallas_call x1, Pallas kernels, shards_fn(): pl.pallas_call(kernel, out_shape=jax.ShapeDtypeStruct((2, 4, 16, 256), jn...  73.3 us

profile of v4, /device:TPU:1, one launch (start us, length us, event | category | flops | bytes accessed | tf_op | source)
XLA Modules:
  0.0 74.8 jit_solution(7236497372158842779)
XLA Ops:
  0.0 73.3 %shard_map.46 = bf16[2,4,16,256]{3,2,1,0:T(8,128)(2,1)} custom-call(bf16[1,16,4096]{2,1,0:T(8,128)(2,1)} %tok_hbm.1, f32[8,8]{1,0:T(8,128)} %coef.1, bf16[1,4096,256]{2,1,0:T(8,128)(2,1)} %gate_hbm.1, bf16[1,4096,256]{2,1,0:T(8,128)(2,1)} %up_hbm.1), custom_call_target="tpu_custom_call" | custom-call | tf_op jit(solution)/shard_map/pallas_call | solution.py:451
  73.3 1.5 %copy.6 = bf16[1,128,256]{2,1,0:T(8,128)(2,1)} copy(bf16[1,128,256]{2,1,0:T(8,128)(2,1)} %bitcast.1) | data formatting | bytes 131072

commit v5 on v4

--- a/solution.py
+++ b/solution.py
@@ -59,7 +59,7 @@
     up_in.start()
 
     barrier = pltpu.get_barrier_semaphore()
-    greeted = [device(dx=1), device(dx=3), device(dy=1), device(dy=3), device(dy=2)]
+    greeted = [device(dx=1), device(dx=3), device(dx=2), device(dy=1), device(dy=3), device(dy=2)]
     greeted += [device(dz=1), device(dz=3), device(dz=2), sibling, partner]
     for one in greeted:
         pl.semaphore_signal(barrier, inc=1, device_id=one, device_id_type=MESH)
@@ -75,6 +75,8 @@
         one = shards(k, 0, fs[0])
         send(one, one, s_a.at[k, 0], on_a(1))
         send(one, one, s_a.at[k, 1], on_a(3))
+        if k == 0:
+            send(one, one, s_a.at[k, 2], on_a(2))
 
     def relay_a(k):
         one = shards(k, 0, fs[1 + k % 2])
@@ -105,7 +107,7 @@
 
     def a(k, j):
         wait(shards(k, 0, fs[j]), s_a.at[k, j - 1])
-        if j == 1 + k % 2:
+        if k > 0 and j == 1 + k % 2:
             relay_a(k)
         if k == 0:
             send_b(0, j)

time: 74.9 us -> 74.8 us (level)
  no operation moved by 1% of the time
where the time goes in v5:
time: 74.8 us; the launch traced here: 74.6 us
  Pallas kernels  73.1 us (98%)
  local copies, waits for them, and re-layouts  1.47 us (2%)
    pallas_call x1, Pallas kernels, shards_fn(): pl.pallas_call(kernel, out_shape=jax.ShapeDtypeStruct((2, 4, 16, 256), jn...  73.1 us

profile of v5, /device:TPU:1, one launch (start us, length us, event | category | flops | bytes accessed | tf_op | source)
XLA Modules:
  0.0 74.6 jit_solution(15892485467652739654)
XLA Ops:
  0.0 73.1 %shard_map.46 = bf16[2,4,16,256]{3,2,1,0:T(8,128)(2,1)} custom-call(bf16[1,16,4096]{2,1,0:T(8,128)(2,1)} %tok_hbm.1, f32[8,8]{1,0:T(8,128)} %coef.1, bf16[1,4096,256]{2,1,0:T(8,128)(2,1)} %gate_hbm.1, bf16[1,4096,256]{2,1,0:T(8,128)(2,1)} %up_hbm.1), custom_call_target="tpu_custom_call" | custom-call | tf_op jit(solution)/shard_map/pallas_call | solution.py:453
  73.1 1.5 %copy.6 = bf16[1,128,256]{2,1,0:T(8,128)(2,1)} copy(bf16[1,128,256]{2,1,0:T(8,128)(2,1)} %bitcast.1) | data formatting | bytes 131072
